TPU v7x, 32 devices: a whole 2x2x4 slice. The times are simulated.
32 devices in a mesh: groups: 2 (over y), chol: 4 (over z), walk: 2 (over x), orb: 2 (over core).
Axes of the slice: x: 2, y: 2, z: 4, core: 2. Of those that a mesh axis runs over, the one named last changes fastest.
Arguments:
- walkers: float32 [32, 2, 36864], P(('groups', 'walk'), None, ('chol', 'orb')), parts along dimension 0, may hold values from -6 to 6
- correlation_inverse: float32 [32, 2, 96, 96], P(('groups', 'walk')), parts along dimension 0, may hold values from -0.625 to 0.625
- half_vectors: bfloat16 [4096, 36864], P(('groups', 'walk'), ('chol', 'orb')), parts along dimension 0, may hold values from -0.01953125 to 0.01953125
- field_vectors: bfloat16 [4096, 384, 384], P(('groups', 'walk'), ('chol', 'orb')), parts along dimension 0, may hold values from -0.0048828125 to 0.0048828125
- samples: float32 [32, 2048], P('groups', 'walk'), parts along dimension 0, may hold values from -6 to 6
- source: int32 [32], P(('groups', 'walk')), parts along dimension 0, may hold values from 0 to 15
Outputs:
- walkers_next: float32 [32, 2, 36864], P(('groups', 'walk'), None, ('chol', 'orb')), parts along dimension 0
There are 2 independent parts, one for each index of `groups`. A program takes and returns all parts, laid end to end along the dimension named above; each array names one. Nothing has to cross between parts.
All inputs are finite; a program needn't handle non-finite values.
Results may differ from a plain program's by a relative error of at most 0.02.
Values may be sent and summed in bfloat16 or wider, within the bound.
No kernel may reach another device: no remote copies, remote signals or barrier semaphores. Data moves between devices by JAX's collectives and lax.ppermute only.
A program may use at most 128 MiB of HBM per device.

v0:
```python
import jax
import jax.numpy as jnp
from jax import lax
from jax.sharding import PartitionSpec as P

TERMS = 4
NS_STEPS = 2


def for_sending(shard):
    return jax.tree.map(lambda a: a.astype(jnp.bfloat16) if a.dtype == jnp.float32 else a, shard)


def complex_product(left_real, left_imag, right_real, right_imag, formula):
    first = jnp.einsum(formula, left_real, right_real, precision=lax.Precision.HIGHEST)
    second = jnp.einsum(formula, left_imag, right_imag, precision=lax.Precision.HIGHEST)
    third = jnp.einsum(formula, left_real, right_imag, precision=lax.Precision.HIGHEST)
    fourth = jnp.einsum(formula, left_imag, right_real, precision=lax.Precision.HIGHEST)
    return (first - second, third + fourth)


def normalizer(gram_real, gram_imag):
    electrons = gram_real.shape[-1]
    identity = jnp.eye(electrons, dtype=jnp.float32)
    scale_factor = jnp.trace(gram_real, axis1=1, axis2=2) / electrons
    iter_real = gram_real / scale_factor[:, None, None]
    iter_imag = gram_imag / scale_factor[:, None, None]
    root_real = jnp.broadcast_to(identity, gram_real.shape)
    root_imag = jnp.zeros_like(gram_real)
    for sweep_index in range(NS_STEPS):
        prod_real, prod_imag = complex_product(
            root_real, root_imag, iter_real, iter_imag, "wij,wjk->wik"
        )
        step_real = 1.5 * identity - 0.5 * prod_real
        step_imag = -0.5 * prod_imag
        iter_real, iter_imag = complex_product(
            iter_real, iter_imag, step_real, step_imag, "wij,wjk->wik"
        )
        root_real, root_imag = complex_product(
            step_real, step_imag, root_real, root_imag, "wij,wjk->wik"
        )
    inverse_root = lax.rsqrt(scale_factor)[:, None, None]
    return (root_real * inverse_root, root_imag * inverse_root)


def field_apply(field_block, values):
    next_real = jnp.einsum(
        "wab,wbn->wan", field_block[:, 0], values[:, 0], preferred_element_type=jnp.float32
    )
    next_real = next_real - jnp.einsum(
        "wab,wbn->wan", field_block[:, 1], values[:, 1], preferred_element_type=jnp.float32
    )
    next_imag = jnp.einsum(
        "wab,wbn->wan", field_block[:, 0], values[:, 1], preferred_element_type=jnp.float32
    )
    next_imag = next_imag + jnp.einsum(
        "wab,wbn->wan", field_block[:, 1], values[:, 0], preferred_element_type=jnp.float32
    )
    return jnp.stack([next_real, next_imag], 1)


def body(walkers, correlation_inverse, half_vectors, field_vectors, samples, source):
    local_walkers = walkers.shape[0]
    row_block = field_vectors.shape[1]
    orbitals = field_vectors.shape[2]
    electrons = correlation_inverse.shape[2]
    grid = walkers.reshape(local_walkers, 2, row_block, electrons)
    theta_real, theta_imag = complex_product(
        grid[:, 0], grid[:, 1], correlation_inverse[:, 0], correlation_inverse[:, 1], "wmk,wkn->wmn"
    )
    theta = (
        jnp.stack([theta_real, theta_imag], 1)
        .reshape(local_walkers, 2, row_block * electrons)
        .astype(jnp.bfloat16)
    )
    all_theta = lax.all_gather(theta, "walk", axis=0, tiled=True)
    bias_part = jnp.einsum(
        "wcj,gj->wcg", all_theta, half_vectors, preferred_element_type=jnp.float32
    )
    bias = lax.psum(bias_part, ("chol", "orb"))
    coefficient = jnp.stack([bias[:, 1], samples - bias[:, 0]], 1).astype(jnp.bfloat16)
    field_part = jnp.einsum(
        "wcg,gab->wcab", coefficient, field_vectors, preferred_element_type=jnp.float32
    )
    field = lax.psum_scatter(field_part, "walk", scatter_dimension=0, tiled=True).astype(
        jnp.bfloat16
    )
    devices_rows = lax.axis_size(("chol", "orb"))
    sharers = devices_rows // local_walkers
    col_width = electrons // sharers
    parted = grid.reshape(local_walkers, 2, row_block, sharers, col_width)
    parted = parted.transpose(0, 3, 1, 2, 4).reshape(devices_rows, 2, row_block, col_width)
    columns = lax.all_to_all(
        parted.astype(jnp.bfloat16), ("chol", "orb"), split_axis=0, concat_axis=2, tiled=True
    ).astype(parted.dtype)
    spread = jnp.broadcast_to(field[:, None], (local_walkers, sharers, 2, row_block, orbitals))
    spread = spread.reshape(devices_rows, 2, row_block, orbitals)
    whole_field = lax.all_to_all(spread, ("chol", "orb"), split_axis=0, concat_axis=2, tiled=True)
    current = columns
    col_summed = columns
    for order_index in range(1, TERMS + 1):
        current = field_apply(whole_field, current.astype(jnp.bfloat16)) / order_index
        col_summed = col_summed + current
    returned = lax.all_to_all(
        col_summed.astype(jnp.bfloat16), ("chol", "orb"), split_axis=2, concat_axis=0, tiled=True
    ).astype(col_summed.dtype)
    returned = returned.reshape(local_walkers, sharers, 2, row_block, col_width)
    summed = returned.transpose(0, 2, 3, 1, 4).reshape(local_walkers, 2, row_block, electrons)
    whole = lax.all_gather(summed.astype(jnp.bfloat16), ("chol", "orb"), axis=2, tiled=True).astype(
        summed.dtype
    )
    gram_real, gram_imag = complex_product(
        whole[:, 0], -whole[:, 1], whole[:, 0], whole[:, 1], "wmi,wmj->wij"
    )
    gram_real = gram_real / orbitals
    gram_imag = gram_imag / orbitals
    root_real, root_imag = normalizer(gram_real, gram_imag)
    norm_real, norm_imag = complex_product(
        summed[:, 0], summed[:, 1], root_real, root_imag, "wmk,wkn->wmn"
    )
    normalized = jnp.stack([norm_real, norm_imag], 1).reshape(
        local_walkers, 2, row_block * electrons
    )
    moved = lax.all_gather(for_sending(normalized), "walk", axis=0, tiled=True).astype(
        normalized.dtype
    )
    return jnp.take(moved, source, axis=0)


def solution(mesh):
    placed = (
        P(("groups", "walk"), None, ("chol", "orb")),
        P(("groups", "walk"), None, None, None),
        P(("groups", "walk"), ("chol", "orb")),
        P(("groups", "walk"), ("chol", "orb"), None),
        P("groups", "walk"),
        P(("groups", "walk")),
    )
    return jax.shard_map(
        body,
        mesh=mesh,
        in_specs=placed,
        out_specs=P(("groups", "walk"), None, ("chol", "orb")),
        check_vma=False,
    )
```

profile of v0, /device:TPU:0, one launch (start us, length us, event | category | flops | bytes accessed | tf_op | source)
XLA Modules:
  0.0 241.8 jit_solution(14504771620466679729)
XLA Ops:
  6.5 1.1 copy.45
  7.8 0.5 fusion.37
  8.3 0.5 fusion.41
  8.7 0.5 fusion.29
  9.4 0.5 fusion.28
  10.0 7.5 %all_gather.9 = bf16[16,2,4608]{2,0,1:T(8,128)(2,1)S(1)} all-gather(bf16[8,2,4608]{2,0,1:T(8,128)(2,1)S(1)} %pad_maximum_fusion.1), channel_id=1, replica_groups=mesh['groups'=2,'chol'=4,'walk'=2,'orb'=2] {'walk'}, dimensions={0}, use_global_device_ids=true | all-gather | bytes 442368 | tf_op jit(solution)/shard_map/all_gather | solution.py:76
  17.5 7.2 %fusion.3 = f32[16,2,1024]{2,0,1:T(8,128)} fusion(bf16[16,2,4608]{2,0,1:T(8,128)(2,1)S(1)} %all_gather.9, bf16[1024,4608]{1,0:T(8,128)(2,1)} %param.8), kind=kOutput, calls=%fused_computation.4 | convolution fusion | flops 301989888 | bytes 9863168 | tf_op jit(solution)/shard_map/wcj,gj->wcg/dot_general | solution.py:77
  25.0 56.4 %all-reduce.2.cloned.1.call-done = f32[16,2,1024]{2,0,1:T(8,128)} async-done(((f32[16,2,1024]{2,0,1:T(8,128)}), f32[16,2,1024]{2,0,1:T(8,128)}) %all-reduce.2.cloned.1.call-update) | async-done | bytes 131088 | tf_op jit(solution)/shard_map/psum | solution.py:80
  81.4 0.8 slice.232
  82.2 0.8 fusion.78
  83.1 29.4 %fusion = f32[16,2,48,384]{3,0,2,1:T(8,128)} fusion(bf16[1024,48,384]{2,1,0:T(8,128)(2,1)} %param.9, bf16[16,1,1024]{2,0,1:T(8,128)(2,1)S(1)} %fusion.78, bf16[16,1,1024]{2,0,1:T(8,128)(2,1)S(1)} %slice.232), kind=kOutput, calls=%fused_computation.1 | convolution fusion | flops 1208090624 | bytes 40173568 | tf_op jit(solution)/shard_map/wcg,gab->wcab/dot_general | solution.py:82
  112.5 0.7 copy.46
  113.2 3.4 %all-to-all-start = ((bf16[8,2,48,96]{3,2,1,0:T(8,128)(2,1)}), bf16[8,2,48,96]{3,2,1,0:T(8,128)(2,1)S(1)}, u32[]{:S(2)}, u32[]{:S(2)}) async-start(bf16[8,2,48,96]{3,2,1,0:T(8,128)(2,1)} %copy.46), calls=%async_computation | async-start | bytes 393216 | tf_op jit(solution)/shard_map/all_to_all | solution.py:93
  116.6 29.9 %reduce-scatter.2.cloned.1.call-done = f32[8,2,48,384]{3,0,2,1:T(8,128)} async-done(((f32[16,2,48,384]{3,0,2,1:T(8,128)}), f32[8,2,48,384]{3,0,2,1:T(8,128)}) %reduce-scatter.2.cloned.1.call-update) | async-done | bytes 1179664 | tf_op jit(solution)/shard_map/reduce_scatter | solution.py:85
  146.5 1.3 convert_element_type.82
  147.8 0.9 copy.52
  148.7 4.6 %all-to-all-start.1 = ((bf16[8,2,48,384]{3,2,1,0:T(8,128)(2,1)}), bf16[8,2,48,384]{3,2,1,0:T(8,128)(2,1)S(1)}, u32[]{:S(2)}, u32[]{:S(2)}) async-start(bf16[8,2,48,384]{3,2,1,0:T(8,128)(2,1)} %copy.52), calls=%async_computation.2 | async-start | bytes 1179648 | tf_op jit(solution)/shard_map/all_to_all | solution.py:98
  153.8 16.3 %all-to-all-done.1 = bf16[8,2,48,384]{3,2,1,0:T(8,128)(2,1)S(1)} async-done(((bf16[8,2,48,384]{3,2,1,0:T(8,128)(2,1)}), bf16[8,2,48,384]{3,2,1,0:T(8,128)(2,1)S(1)}, u32[]{:S(2)}, u32[]{:S(2)}) %all-to-all-start.1) | async-done | bytes 589856 | tf_op jit(solution)/shard_map/all_to_all | solution.py:98
  174.4 10.7 %all_to_all.54 = bf16[1,2,384,96]{3,1,0,2:T(2,128)(2,1)S(1)} all-to-all(bf16[1,2,384,96]{3,1,0,2:T(2,128)(2,1)S(1)} %copy.54), channel_id=1, replica_groups=mesh['groups'=2,'chol'=4,'walk'=2,'orb'=2] {'chol','orb'}, dimensions={2} | all-to-all | bytes 294912 | tf_op jit(solution)/shard_map/all_to_all | solution.py:104
  185.2 0.7 copy.56
  186.0 23.3 %all-gather.3.cloned.1.call-done = bf16[8,1,2,384,96]{4,0,2,1,3:T(8,128)(2,1)} async-done(((bf16[8,1,2,48,96]{4,0,2,1,3:T(8,128)(2,1)}), bf16[8,1,2,384,96]{4,0,2,1,3:T(8,128)(2,1)}) %all-gather.3.cloned.1.call-update) | async-done | bytes 1179664 | tf_op jit(solution)/shard_map/all_gather | solution.py:109
  209.3 2.1 copy.57
  211.4 0.8 fusion.18
  212.2 0.8 fusion.16
  213.1 0.4 select_reduce_fusion
  213.9 0.5 fusion.62
  214.5 0.5 fusion.58
  214.9 0.5 fusion.15
  215.4 0.5 fusion.60
  215.9 0.6 fusion.88
  216.5 0.5 fusion.52
  217.0 0.5 fusion.13
  217.5 0.6 fusion.87
  218.1 0.5 convolution_subtract_fusion.4
  218.6 0.5 convolution_subtract_fusion.3
  219.1 0.5 convolution_add_fusion.4
  219.6 0.5 convolution_add_fusion.3
  220.2 0.5 fusion.89
  220.7 0.5 fusion.91
  221.2 0.5 fusion.12
  221.8 0.5 fusion.92
  222.3 0.5 fusion.90
  222.9 0.5 fusion.10
  223.4 0.5 fusion.8
  223.9 0.8 fusion.9
  226.7 6.6 %all_gather.11 = bf16[16,2,4608]{2,1,0:T(2,128)(2,1)S(1)} all-gather(bf16[8,2,4608]{2,1,0:T(2,128)(2,1)S(1)} %pad_maximum_fusion.2), channel_id=1, replica_groups=mesh['groups'=2,'chol'=4,'walk'=2,'orb'=2] {'walk'}, dimensions={0}, use_global_device_ids=true | all-gather | bytes 442368 | tf_op jit(solution)/shard_map/all_gather | solution.py:124
  233.5 0.9 gather_fusion
  234.4 0.9 broadcast_select_fusion
  (59 shorter events, 8.0 us)
Async XLA Ops:
  6.5 1.3 copy-start
  6.5 74.9 %all-reduce.2.cloned.1.call-start = ((), (), s32[]{:S(2)}) async-start(), calls=%async_computation.4 | async-start | bytes 262144 | tf_op jit(solution)/shard_map/psum | solution.py:80
  17.5 64.7 %copy-start.1 = (f32[16,1024]{1,0:T(8,128)S(1)}, f32[16,1024]{1,0:T(8,128)}, u32[]{:S(2)}) copy-start(f32[16,1024]{1,0:T(8,128)} %param.10) | copy-start | bytes 196612
  24.7 121.7 %reduce-scatter.2.cloned.1.call-start = ((), (), s32[]{:S(2)}) async-start(), calls=%async_computation.5 | async-start | bytes 3538944 | tf_op jit(solution)/shard_map/reduce_scatter | solution.py:85
  113.2 35.5 %all-to-all-start = ((bf16[8,2,48,96]{3,2,1,0:T(8,128)(2,1)}), bf16[8,2,48,96]{3,2,1,0:T(8,128)(2,1)S(1)}, u32[]{:S(2)}, u32[]{:S(2)}) async-start(bf16[8,2,48,96]{3,2,1,0:T(8,128)(2,1)} %copy.46), calls=%async_computation | async-start | bytes 393216 | tf_op jit(solution)/shard_map/all_to_all | solution.py:93
  148.7 21.4 %all-to-all-start.1 = ((bf16[8,2,48,384]{3,2,1,0:T(8,128)(2,1)}), bf16[8,2,48,384]{3,2,1,0:T(8,128)(2,1)S(1)}, u32[]{:S(2)}, u32[]{:S(2)}) async-start(bf16[8,2,48,384]{3,2,1,0:T(8,128)(2,1)} %copy.52), calls=%async_computation.2 | async-start | bytes 1179648 | tf_op jit(solution)/shard_map/all_to_all | solution.py:98
  153.3 56.0 %all-gather.3.cloned.1.call-start = ((), (), s32[]{:S(2)}) async-start(), calls=%async_computation.6 | async-start | bytes 1769472 | tf_op jit(solution)/shard_map/all_gather | solution.py:109
  174.2 11.7 %copy-start.2 = (s32[8]{0:T(128)S(1)}, s32[8]{0:T(128)}, u32[]{:S(2)}) copy-start(s32[8]{0:T(128)} %param.11) | copy-start | bytes 100
Sparse Core Ops, SparseCore 0:
  24.8 56.5 all-reduce.1
  112.6 33.8 reduce-scatter.1
  186.0 23.2 all-gather.2
where the time goes:
time: 242 us
  waiting for transfers between devices  126 us (52%)
  matrix products  56.8 us (23%)
  blocking collectives  24.8 us (10%)
  between operations  13.6 us (6%)
  starting transfers between devices  8.5 us (4%)
  local copies, waits for them, and re-layouts  8.36 us (3%)
  other arithmetic  3.9 us (2%)
    psum x1, waiting for transfers between devices, body(): bias = lax.psum(bias_part, ('chol', 'orb'))  56.4 us
    reduce_scatter x1, waiting for transfers between devices, body(): lax.psum_scatter(field_part, 'walk', scatter_dimension=0, tiled=True)  29.9 us
    dot_general x1, matrix products, body(): jnp.einsum('wcg,gab->wcab', coefficient, field_vectors, preferred_element...  29.4 us
    all_gather x1, waiting for transfers between devices, body(): lax.all_gather(summed.astype(jnp.bfloat16), ('chol', 'orb'), axis=2, tile...  23.3 us
    all_to_all x1, waiting for transfers between devices, body(): lax.all_to_all(spread, ('chol', 'orb'), split_axis=0, concat_axis=2, tile...  16.3 us
    all_to_all x1, blocking collectives, body(): lax.all_to_all(col_summed.astype(jnp.bfloat16), ('chol', 'orb'), split_ax...  10.7 us
    all_gather x1, blocking collectives, body(): all_theta = lax.all_gather(theta, 'walk', axis=0, tiled=True)  7.47 us
    dot_general x1, matrix products, body(): jnp.einsum('wcj,gj->wcg', all_theta, half_vectors, preferred_element_type...  7.2 us
  transfers between devices with their start and end apart: 5, of which 4 were waited for; matrix products, arithmetic and copies ran while one was open for 1% of the time, Pallas kernels for 0%

commit v1 on v0

--- a/solution.py
+++ b/solution.py
@@ -77,7 +77,11 @@
     bias_part = jnp.einsum(
         "wcj,gj->wcg", all_theta, half_vectors, preferred_element_type=jnp.float32
     )
-    bias = lax.psum(bias_part, ("chol", "orb"))
+
+    def enter_sides(unit):
+        return jnp.sum(jax.lax.all_gather(unit, ("chol", "orb")), axis=0)
+
+    bias = enter_sides(bias_part)
     coefficient = jnp.stack([bias[:, 1], samples - bias[:, 0]], 1).astype(jnp.bfloat16)
     field_part = jnp.einsum(
         "wcg,gab->wcab", coefficient, field_vectors, preferred_element_type=jnp.float32

time: 242 us -> 210 us (0.87)
  waiting for transfers between devices: 126 us -> 93.7 us
    psum x1 -> x0, waiting for transfers between devices: 56.4 us -> none  [body(): bias = lax.psum(bias_part, ('chol', 'orb'))]
    all_gather x0 -> x1, waiting for transfers between devices: none -> 23.7 us  [enter_sides(): return jnp.sum(jax.lax.all_gather(unit, ('chol', 'orb')), axis=0)]
  transfers between devices with their start and end apart: 5 -> 5, of which waited for: 4 -> 4; matrix products, arithmetic and copies ran while one was open for 1% -> 2% of each run, Pallas kernels for 0% -> 0%
where the time goes in v1:
time: 210 us; the launch traced here: 209 us
  waiting for transfers between devices  93.7 us (45%)
  matrix products  56.8 us (27%)
  blocking collectives  24.8 us (12%)
  between operations  13.6 us (6%)
  starting transfers between devices  8.48 us (4%)
  local copies, waits for them, and re-layouts  7.53 us (4%)
  other arithmetic  4.35 us (2%)
    reduce_scatter x1, waiting for transfers between devices, body(): lax.psum_scatter(field_part, 'walk', scatter_dimension=0, tiled=True)  30.4 us
    dot_general x1, matrix products, body(): jnp.einsum('wcg,gab->wcab', coefficient, field_vectors, preferred_element...  29.4 us
    all_gather x1, waiting for transfers between devices, enter_sides(): return jnp.sum(jax.lax.all_gather(unit, ('chol', 'orb')), axis=0)  23.7 us
    all_gather x1, waiting for transfers between devices, body(): lax.all_gather(summed.astype(jnp.bfloat16), ('chol', 'orb'), axis=2, tile...  23.3 us
    all_to_all x1, waiting for transfers between devices, body(): lax.all_to_all(spread, ('chol', 'orb'), split_axis=0, concat_axis=2, tile...  16.3 us
    all_to_all x1, blocking collectives, body(): lax.all_to_all(col_summed.astype(jnp.bfloat16), ('chol', 'orb'), split_ax...  10.7 us
    all_gather x1, blocking collectives, body(): all_theta = lax.all_gather(theta, 'walk', axis=0, tiled=True)  7.47 us
    dot_general x1, matrix products, body(): jnp.einsum('wcj,gj->wcg', all_theta, half_vectors, preferred_element_type...  7.17 us
  transfers between devices with their start and end apart: 5, of which 4 were waited for; matrix products, arithmetic and copies ran while one was open for 2% of the time, Pallas kernels for 0%

profile of v1, /device:TPU:0, one launch (start us, length us, event | category | flops | bytes accessed | tf_op | source)
XLA Modules:
  0.0 209.2 jit_solution(9347680050240189926)
XLA Ops:
  6.5 1.1 copy.45
  7.8 0.5 fusion.37
  8.3 0.5 fusion.41
  8.7 0.5 fusion.29
  9.4 0.5 fusion.28
  10.0 7.5 %all_gather.15 = bf16[16,2,4608]{2,0,1:T(8,128)(2,1)S(1)} all-gather(bf16[8,2,4608]{2,0,1:T(8,128)(2,1)S(1)} %pad_maximum_fusion.1), channel_id=1, replica_groups=mesh['groups'=2,'chol'=4,'walk'=2,'orb'=2] {'walk'}, dimensions={0}, use_global_device_ids=true | all-gather | bytes 442368 | tf_op jit(solution)/shard_map/all_gather | solution.py:76
  17.5 7.2 %fusion.3 = f32[16,2,1024]{2,0,1:T(8,128)} fusion(bf16[16,2,4608]{2,0,1:T(8,128)(2,1)S(1)} %all_gather.15, bf16[1024,4608]{1,0:T(8,128)(2,1)} %param.8), kind=kOutput, calls=%fused_computation.4 | convolution fusion | flops 301989888 | bytes 9863168 | tf_op jit(solution)/shard_map/wcj,gj->wcg/dot_general | solution.py:77
  24.9 23.7 %all-gather.5.cloned.1.call-done = f32[128,2,1024]{2,0,1:T(8,128)} async-done(((f32[16,2,1024]{2,0,1:T(8,128)}), f32[128,2,1024]{2,0,1:T(8,128)}) %all-gather.5.cloned.1.call-update) | async-done | bytes 1048592 | tf_op jit(solution)/shard_map/all_gather | solution.py:82
  48.6 1.3 reduce_sum.19
  49.9 29.4 %fusion = f32[16,2,48,384]{3,0,2,1:T(8,128)} fusion(bf16[1024,48,384]{2,1,0:T(8,128)(2,1)} %param.9, bf16[16,1,1024]{2,0,1:T(8,128)(2,1)S(1)} %fusion.78, bf16[16,1,1024]{2,0,1:T(8,128)(2,1)S(1)} %slice.232), kind=kOutput, calls=%fused_computation.1 | convolution fusion | flops 1208090624 | bytes 40173568 | tf_op jit(solution)/shard_map/wcg,gab->wcab/dot_general | solution.py:86
  79.4 0.7 copy.46
  80.1 3.4 %all-to-all-start = ((bf16[8,2,48,96]{3,2,1,0:T(8,128)(2,1)}), bf16[8,2,48,96]{3,2,1,0:T(8,128)(2,1)S(1)}, u32[]{:S(2)}, u32[]{:S(2)}) async-start(bf16[8,2,48,96]{3,2,1,0:T(8,128)(2,1)} %copy.46), calls=%async_computation | async-start | bytes 393216 | tf_op jit(solution)/shard_map/all_to_all | solution.py:97
  83.5 30.4 %reduce-scatter.2.cloned.1.call-done = f32[8,2,48,384]{3,0,2,1:T(8,128)} async-done(((f32[16,2,48,384]{3,0,2,1:T(8,128)}), f32[8,2,48,384]{3,0,2,1:T(8,128)}) %reduce-scatter.2.cloned.1.call-update) | async-done | bytes 1179664 | tf_op jit(solution)/shard_map/reduce_scatter | solution.py:89
  113.9 1.3 convert_element_type.82
  115.2 0.9 copy.52
  116.1 4.6 %all-to-all-start.1 = ((bf16[8,2,48,384]{3,2,1,0:T(8,128)(2,1)}), bf16[8,2,48,384]{3,2,1,0:T(8,128)(2,1)S(1)}, u32[]{:S(2)}, u32[]{:S(2)}) async-start(bf16[8,2,48,384]{3,2,1,0:T(8,128)(2,1)} %copy.52), calls=%async_computation.2 | async-start | bytes 1179648 | tf_op jit(solution)/shard_map/all_to_all | solution.py:102
  121.2 16.3 %all-to-all-done.1 = bf16[8,2,48,384]{3,2,1,0:T(8,128)(2,1)S(1)} async-done(((bf16[8,2,48,384]{3,2,1,0:T(8,128)(2,1)}), bf16[8,2,48,384]{3,2,1,0:T(8,128)(2,1)S(1)}, u32[]{:S(2)}, u32[]{:S(2)}) %all-to-all-start.1) | async-done | bytes 589856 | tf_op jit(solution)/shard_map/all_to_all | solution.py:102
  141.8 10.7 %all_to_all.54 = bf16[1,2,384,96]{3,1,0,2:T(2,128)(2,1)S(1)} all-to-all(bf16[1,2,384,96]{3,1,0,2:T(2,128)(2,1)S(1)} %copy.54), channel_id=1, replica_groups=mesh['groups'=2,'chol'=4,'walk'=2,'orb'=2] {'chol','orb'}, dimensions={2} | all-to-all | bytes 294912 | tf_op jit(solution)/shard_map/all_to_all | solution.py:108
  152.6 0.7 copy.56
  153.4 23.3 %all-gather.7.cloned.1.call-done = bf16[8,1,2,384,96]{4,0,2,1,3:T(8,128)(2,1)} async-done(((bf16[8,1,2,48,96]{4,0,2,1,3:T(8,128)(2,1)}), bf16[8,1,2,384,96]{4,0,2,1,3:T(8,128)(2,1)}) %all-gather.7.cloned.1.call-update) | async-done | bytes 1179664 | tf_op jit(solution)/shard_map/all_gather | solution.py:113
  176.7 2.1 copy.57
  178.8 0.8 fusion.18
  179.6 0.8 fusion.16
  180.5 0.4 select_reduce_fusion
  180.9 0.4 fusion.7
  181.3 0.5 fusion.62
  181.8 0.5 fusion.58
  182.3 0.5 fusion.15
  182.8 0.5 fusion.60
  183.3 0.6 fusion.88
  183.9 0.5 fusion.52
  184.4 0.5 fusion.13
  184.9 0.6 fusion.87
  185.5 0.5 convolution_subtract_fusion.4
  186.0 0.5 convolution_subtract_fusion.3
  186.5 0.5 convolution_add_fusion.4
  187.0 0.5 convolution_add_fusion.3
  187.5 0.5 fusion.89
  188.1 0.5 fusion.91
  188.6 0.5 fusion.12
  189.1 0.5 fusion.92
  189.7 0.5 fusion.90
  190.2 0.5 fusion.10
  190.8 0.5 fusion.8
  191.3 0.8 fusion.9
  194.1 6.6 %all_gather.19 = bf16[16,2,4608]{2,1,0:T(2,128)(2,1)S(1)} all-gather(bf16[8,2,4608]{2,1,0:T(2,128)(2,1)S(1)} %pad_maximum_fusion.2), channel_id=1, replica_groups=mesh['groups'=2,'chol'=4,'walk'=2,'orb'=2] {'walk'}, dimensions={0}, use_global_device_ids=true | all-gather | bytes 442368 | tf_op jit(solution)/shard_map/all_gather | solution.py:128
  200.9 0.9 gather_fusion
  201.8 0.9 broadcast_select_fusion
  (60 shorter events, 7.7 us)
Async XLA Ops:
  6.5 1.3 copy-start
  6.5 42.1 %all-gather.5.cloned.1.call-start = ((), (), s32[]{:S(2)}) async-start(), calls=%async_computation.5 | async-start | bytes 1179648 | tf_op jit(solution)/shard_map/all_gather | solution.py:82
  24.7 25.2 %copy-start.1 = (f32[16,1024]{1,0:T(8,128)S(1)}, f32[16,1024]{1,0:T(8,128)}, u32[]{:S(2)}) copy-start(f32[16,1024]{1,0:T(8,128)} %param.10) | copy-start | bytes 196612
  24.7 89.2 %reduce-scatter.2.cloned.1.call-start = ((), (), s32[]{:S(2)}) async-start(), calls=%async_computation.4 | async-start | bytes 3538944 | tf_op jit(solution)/shard_map/reduce_scatter | solution.py:89
  80.1 36.0 %all-to-all-start = ((bf16[8,2,48,96]{3,2,1,0:T(8,128)(2,1)}), bf16[8,2,48,96]{3,2,1,0:T(8,128)(2,1)S(1)}, u32[]{:S(2)}, u32[]{:S(2)}) async-start(bf16[8,2,48,96]{3,2,1,0:T(8,128)(2,1)} %copy.46), calls=%async_computation | async-start | bytes 393216 | tf_op jit(solution)/shard_map/all_to_all | solution.py:97
  116.1 21.3 %all-to-all-start.1 = ((bf16[8,2,48,384]{3,2,1,0:T(8,128)(2,1)}), bf16[8,2,48,384]{3,2,1,0:T(8,128)(2,1)S(1)}, u32[]{:S(2)}, u32[]{:S(2)}) async-start(bf16[8,2,48,384]{3,2,1,0:T(8,128)(2,1)} %copy.52), calls=%async_computation.2 | async-start | bytes 1179648 | tf_op jit(solution)/shard_map/all_to_all | solution.py:102
  120.7 56.0 %all-gather.7.cloned.1.call-start = ((), (), s32[]{:S(2)}) async-start(), calls=%async_computation.6 | async-start | bytes 1769472 | tf_op jit(solution)/shard_map/all_gather | solution.py:113
  141.6 11.7 %copy-start.2 = (s32[8]{0:T(128)S(1)}, s32[8]{0:T(128)}, u32[]{:S(2)}) copy-start(s32[8]{0:T(128)} %param.11) | copy-start | bytes 100
Sparse Core Ops, SparseCore 0:
  24.8 23.7 all-gather.4
  79.5 34.3 reduce-scatter.1
  153.4 23.2 all-gather.6
